TPU v7x, 32 devices: a whole 2x2x4 slice. The times are simulated.
32 devices in a mesh: ctx: 16 (over z, y, core), heads: 2 (over x).
Axes of the slice: x: 2, y: 2, z: 4, core: 2. Of those that a mesh axis runs over, the one named last changes fastest.
Arguments:
- activations: bfloat16 [5376, 16384], P('heads', 'ctx'), may hold values from -6 to 6
- frozen_query_rows: bfloat16 [16384, 4096], P('ctx', 'heads'), may hold values from -100 to 100
- frozen_key_rows: bfloat16 [16384, 2048], P('ctx', 'heads'), may hold values from -6 to 6
- frozen_value_rows: bfloat16 [16384, 2048], P('ctx', 'heads'), may hold values from -6 to 6
- output_gradient: bfloat16 [16384, 4096], P('ctx', 'heads'), may hold values from -0.5 to 0.5
- query_down_weight: bfloat16 [5376, 16], P('heads'), may hold values from -0.078125 to 0.078125
- query_up_weight: bfloat16 [16, 4096], P(None, 'heads'), may hold values from -0.0390625 to 0.0390625
- key_down_weight: bfloat16 [5376, 16], P('heads'), may hold values from -0.078125 to 0.078125
- key_up_weight: bfloat16 [16, 2048], P(None, 'heads'), may hold values from -0.0390625 to 0.0390625
- value_down_weight: bfloat16 [5376, 16], P('heads'), may hold values from -0.078125 to 0.078125
- value_up_weight: bfloat16 [16, 2048], P(None, 'heads'), may hold values from -0.0390625 to 0.0390625
Outputs:
- query_down_gradient: float32 [5376, 16], P('heads')
- query_up_gradient: float32 [16, 4096], P(None, 'heads')
- key_down_gradient: float32 [5376, 16], P('heads')
- key_up_gradient: float32 [16, 2048], P(None, 'heads')
- value_down_gradient: float32 [5376, 16], P('heads')
- value_up_gradient: float32 [16, 2048], P(None, 'heads')
All inputs are finite; a program needn't handle non-finite values.
Results may differ from a plain program's by a relative error of at most 0.0098.
Values may be sent and summed in bfloat16 or wider, within the bound.
No kernel may reach another device: no remote copies, remote signals or barrier semaphores. Data moves between devices by JAX's collectives and lax.ppermute only.
A program may use at most 256 MiB of HBM per device.

v0:
```python
import jax
import jax.numpy as jnp
from jax import lax
from jax.sharding import PartitionSpec as P

HEAD_WIDTH = 128
WINDOW = 1024


adapter_scale = 2.0
highest_precision = lax.Precision.HIGHEST


def shifted(shard, axis, by):
    length = lax.axis_size(axis)
    pairs = [(i, i + by) for i in range(length) if 0 <= i + by < length]
    return lax.ppermute(shard, axis, pairs)


def band_grad(query_matrix, key_rows, value_rows, output_gradient, offset, leading):
    rows_here = query_matrix.shape[0]
    span = key_rows.shape[0]
    window = span - rows_here
    head_size = HEAD_WIDTH
    kv_heads = key_rows.shape[1] // head_size
    query_group_width = query_matrix.shape[1] // (kv_heads * head_size)
    scale = head_size ** (-0.5)
    query_heads = query_matrix.reshape(rows_here, kv_heads, query_group_width, head_size)
    key_heads = key_rows.reshape(span, kv_heads, head_size)
    value_heads = value_rows.reshape(span, kv_heads, head_size)
    grad_heads = output_gradient.reshape(rows_here, kv_heads, query_group_width, head_size)
    scores = scale * jnp.einsum(
        "qhgd,khd->hgqk", query_heads, key_heads, preferred_element_type=jnp.float32
    )
    query_pos = jnp.arange(rows_here, dtype=jnp.int32)[:, None]
    key_pos = jnp.arange(span, dtype=jnp.int32)[None, :]
    allowed = (key_pos > query_pos) & (key_pos <= query_pos + window)
    allowed = allowed & ((key_pos + offset >= window) | jnp.logical_not(leading))
    scores = jnp.where(allowed, scores, -jnp.inf)
    highest_score = jnp.max(scores, axis=-1, keepdims=True)
    exponent = jnp.exp(scores - highest_score)
    weights = exponent / jnp.sum(exponent, axis=-1, keepdims=True)
    weights_low = weights.astype(jnp.bfloat16)
    attended = jnp.einsum(
        "hgqk,khd->qhgd", weights_low, value_heads, preferred_element_type=jnp.float32
    )
    row_dots = jnp.transpose(jnp.sum(grad_heads.astype(jnp.float32) * attended, axis=-1), (1, 2, 0))
    grad_weights = jnp.einsum(
        "qhgd,khd->hgqk", grad_heads, value_heads, preferred_element_type=jnp.float32
    )
    grad_low = (scale * weights * (grad_weights - row_dots[..., None])).astype(jnp.bfloat16)
    query_gradient_rows = jnp.einsum(
        "hgqk,khd->qhgd", grad_low, key_heads, preferred_element_type=jnp.float32
    )
    key_gradient_rows = jnp.einsum(
        "hgqk,qhgd->khd", grad_low, query_heads, preferred_element_type=jnp.float32
    )
    value_gradient_rows = jnp.einsum(
        "hgqk,qhgd->khd", weights_low, grad_heads, preferred_element_type=jnp.float32
    )
    return (
        query_gradient_rows.reshape(rows_here, -1),
        key_gradient_rows.reshape(span, -1),
        value_gradient_rows.reshape(span, -1),
    )


def adapted_output(base_output, rank_portion, adapter_up_weight):
    lifted_rows = jnp.dot(
        rank_portion, adapter_up_weight.astype(jnp.float32), precision=highest_precision
    )
    return (base_output.astype(jnp.float32) + adapter_scale * lifted_rows).astype(jnp.bfloat16)


def project_rows(gradient_rows, adapter_up_weight):
    return jnp.dot(
        gradient_rows, adapter_up_weight.astype(jnp.float32).T, precision=highest_precision
    )


def on_device(
    activations,
    frozen_query_rows,
    frozen_key_rows,
    frozen_value_rows,
    output_gradient,
    query_down_weight,
    query_up_weight,
    key_down_weight,
    key_up_weight,
    value_down_weight,
    value_up_weight,
):
    rank_width = query_down_weight.shape[1]
    tokens = activations.shape[1]
    window = WINDOW
    adapter_weights_all = jnp.concatenate(
        [query_down_weight, key_down_weight, value_down_weight], axis=1
    )
    partial_rank = lax.dot_general(
        activations,
        adapter_weights_all,
        (((0,), (0,)), ((), ())),
        preferred_element_type=jnp.float32,
    )
    rank_all = lax.psum(partial_rank, "heads")
    query_rank_rows = rank_all[:, :rank_width]
    key_rank_rows = rank_all[:, rank_width : 2 * rank_width]
    value_rank_rows = rank_all[:, 2 * rank_width :]
    query_matrix = adapted_output(frozen_query_rows, query_rank_rows, query_up_weight)
    key_rows = adapted_output(frozen_key_rows, key_rank_rows, key_up_weight)
    value_rows = adapted_output(frozen_value_rows, value_rank_rows, value_up_weight)
    prior_keys, prior_values = shifted((key_rows, value_rows), "ctx", 1)
    span_keys = jnp.concatenate([prior_keys, key_rows], axis=0)
    span_values = jnp.concatenate([prior_values, value_rows], axis=0)
    leading = lax.axis_index("ctx") == 0
    block_rows = min(512, tokens)
    width_k = key_rows.shape[1]

    def advance(carried, block_index):
        sum_keys, sum_values = carried
        offset = block_index * block_rows
        query_rows = lax.dynamic_slice_in_dim(query_matrix, offset, block_rows, 0)
        grad_rows = lax.dynamic_slice_in_dim(output_gradient, offset, block_rows, 0)
        key_span = lax.dynamic_slice_in_dim(span_keys, offset, block_rows + window, 0)
        value_span = lax.dynamic_slice_in_dim(span_values, offset, block_rows + window, 0)
        query_gradient_rows, key_gradient_rows, value_gradient_rows = band_grad(
            query_rows, key_span, value_span, grad_rows, offset, leading
        )
        sum_keys = lax.dynamic_update_slice_in_dim(
            sum_keys,
            lax.dynamic_slice_in_dim(sum_keys, offset, block_rows + window, 0) + key_gradient_rows,
            offset,
            0,
        )
        sum_values = lax.dynamic_update_slice_in_dim(
            sum_values,
            lax.dynamic_slice_in_dim(sum_values, offset, block_rows + window, 0)
            + value_gradient_rows,
            offset,
            0,
        )
        return ((sum_keys, sum_values), query_gradient_rows)

    empty = jnp.zeros((window + tokens, width_k), jnp.float32)
    (sum_keys, sum_values), grad_blocks = lax.scan(
        advance, (empty, empty), jnp.arange(tokens // block_rows, dtype=jnp.int32)
    )
    query_gradient_rows = grad_blocks.reshape(tokens, -1)
    earlier_keys = sum_keys[:window]
    earlier_values = sum_values[:window]
    local_key_rows = sum_keys[window:]
    local_value_rows = sum_values[window:]
    prior_rank = shifted(rank_all[tokens - window :, rank_width:], "ctx", 1)
    partial_inner = jnp.concatenate(
        [
            project_rows(query_gradient_rows, query_up_weight),
            project_rows(local_key_rows, key_up_weight),
            project_rows(local_value_rows, value_up_weight),
        ],
        axis=1,
    )
    partial_prior = jnp.concatenate(
        [project_rows(earlier_keys, key_up_weight), project_rows(earlier_values, value_up_weight)],
        axis=1,
    )
    inner_function, inner_prior = lax.psum((partial_inner, partial_prior), "heads")
    inner_back = shifted(inner_prior, "ctx", -1)
    inner_function = inner_function + jnp.pad(inner_back, ((tokens - window, 0), (rank_width, 0)))
    key_up_gradient = adapter_scale * (
        jnp.dot(key_rank_rows.T, local_key_rows, precision=highest_precision)
        + jnp.dot(prior_rank[:, :rank_width].T, earlier_keys, precision=highest_precision)
    )
    value_up_gradient = adapter_scale * (
        jnp.dot(value_rank_rows.T, local_value_rows, precision=highest_precision)
        + jnp.dot(prior_rank[:, rank_width:].T, earlier_values, precision=highest_precision)
    )
    query_up_gradient = adapter_scale * jnp.dot(
        query_rank_rows.T, query_gradient_rows, precision=highest_precision
    )
    widened_input_rows = activations.astype(jnp.float32)
    query_down_gradient = adapter_scale * jnp.dot(
        widened_input_rows, inner_function[:, :rank_width], precision=highest_precision
    )
    key_down_gradient = adapter_scale * jnp.dot(
        widened_input_rows,
        inner_function[:, rank_width : 2 * rank_width],
        precision=highest_precision,
    )
    value_down_gradient = adapter_scale * jnp.dot(
        widened_input_rows, inner_function[:, 2 * rank_width :], precision=highest_precision
    )
    results = lax.psum(
        (
            query_down_gradient,
            query_up_gradient,
            key_down_gradient,
            key_up_gradient,
            value_down_gradient,
            value_up_gradient,
        ),
        "ctx",
    )
    return results


def solution(mesh):
    in_specs = (
        P("heads", "ctx"),
        P("ctx", "heads"),
        P("ctx", "heads"),
        P("ctx", "heads"),
        P("ctx", "heads"),
        P("heads", None),
        P(None, "heads"),
        P("heads", None),
        P(None, "heads"),
        P("heads", None),
        P(None, "heads"),
    )
    out_specs = (
        P("heads", None),
        P(None, "heads"),
        P("heads", None),
        P(None, "heads"),
        P("heads", None),
        P(None, "heads"),
    )
    return jax.shard_map(
        on_device, mesh=mesh, in_specs=in_specs, out_specs=out_specs, check_vma=False
    )
```

profile of v0, /device:TPU:0, one launch (start us, length us, event | category | flops | bytes accessed | tf_op | source)
XLA Modules:
  0.0 669.2 jit_solution(3086470698611373689)
XLA Ops:
  11.9 25.2 %all-reduce.7.cloned.1.call-done = f32[1024,48]{0,1:T(8,128)} async-done(((f32[1024,48]{0,1:T(8,128)}), f32[1024,48]{0,1:T(8,128)}) %all-reduce.7.cloned.1.call-update) | async-done | bytes 196624 | tf_op jit(solution)/shard_map/psum | solution.py:106
  54.5 7.0 %add_convert_fusion = bf16[1024,2048]{1,0:T(8,128)(2,1)} fusion(bf16[1024,2048]{1,0:T(8,128)(2,1)} %param.14, bf16[16,2048]{1,0:T(8,128)(2,1)S(1)} %copy-done, f32[1024,48]{0,1:T(8,128)S(1)} %copy-done.5), kind=kOutput, calls=%fused_computation.33 | convolution fusion | flops 411041792 | bytes 8519680 | tf_op jit(solution)/shard_map/dot_general | solution.py:69
  79.4 385.9 %while.16 = (s32[]{:T(128)}, f32[2048,1024]{0,1:T(8,128)}, f32[2048,1024]{0,1:T(8,128)}, f32[2,512,2048]{2,1,0:T(8,128)}, s32[2]{0:T(128)}, /*index=5*/bf16[1024...) while((s32[]{:T(128)}, f32[2048,1024]{0,1:T(8,128)}, ...), condition=%wide.region_5.6_spmd, body=%wide.region_1.5_spmd.sunk | while | flops 19475200000 | bytes 467311968 | solution.py:146
  113.0 24.5 %fusion.132 = (f32[8,2,512]{2,1,0:T(2,128)S(1)}, f32[8,2,512,1536]{2,3,1,0:T(8,128)}) fusion(pred[512,1536]{0,1:T(8,128)(4,1)S(1)} %fusion.131, bf16[1536,8,128,1]{0,2,3,1:T(8,128)(2,1)} %bitcast.149, bf16[512,8,2,128]{0,3,2,1:T(8,128)(2,1)} %bitcast.151), kind=kOutput, calls=%fused_computation.86.clone.1 | convolution fusion | flops 3271558656 | bytes 56393728 | tf_op jit(solution)/shard_map/while/body/eval_jaxpr/sub | solution.py:41
  137.5 27.4 %fusion.133 = bf16[8,2,512,1536]{2,3,1,0:T(8,128)(2,1)} fusion(f32[8,2,512,1536]{2,3,1,0:T(8,128)} %get-tuple-element.234, f32[8,2,512]{2,1,0:T(2,128)S(1)} %get-tuple-element.235), kind=kLoop, calls=%fused_computation.11.clone.1 | loop fusion | flops 25165824 | bytes 75530240 | tf_op jit(solution)/shard_map/while/body/eval_jaxpr/convert_element_type | solution.py:43
  165.0 12.6 %fusion.135 = f32[512,8,2]{0,2,1:T(2,128)S(1)} fusion(bf16[512,8,2,128]{0,3,2,1:T(8,128)(2,1)S(1)} %bitcast.141, bf16[1536,8,128,1]{0,2,3,1:T(8,128)(2,1)} %bitcast.147, bf16[8,2,512,1536]{2,3,1,0:T(8,128)(2,1)} %fusion.133), kind=kOutput, calls=%fused_computation.18.clone.1 | convolution fusion | flops 3224363008 | bytes 30441472 | tf_op jit(solution)/shard_map/while/body/eval_jaxpr/hgqk,khd->qhgd/dot_general | solution.py:44
  177.6 14.4 %fusion.134 = f32[8,128,1536,1]{2,1,3,0:T(8,128)} fusion(bf16[512,8,2,128]{0,3,2,1:T(8,128)(2,1)S(1)} %bitcast.142, bf16[8,2,512,1536]{2,3,1,0:T(8,128)(2,1)} %fusion.133), kind=kOutput, calls=%fused_computation.88.clone.1 | convolution fusion | flops 3221225472 | bytes 33554432 | tf_op jit(solution)/shard_map/while/body/eval_jaxpr/hgqk,qhgd->khd/dot_general | solution.py:58
  192.0 25.9 %fusion.136 = bf16[8,2,512,1536]{2,3,1,0:T(8,128)(2,1)} fusion(bf16[1536,8,128,1]{0,2,3,1:T(8,128)(2,1)} %bitcast.148, bf16[512,8,2,128]{0,3,2,1:T(8,128)(2,1)S(1)} %bitcast.143, f32[8,2,512]{2,1,0:T(2,128)S(1)} %bitcast.157, f32[8,2,512,1536]{2,3,1,0:T(8,128)} %get-tuple-element.234, f32[8,2,512]{2,1,0:T(2,128)S(1)} %get-tuple-element.235), kind=kOutput, calls=%fused_computation.3.clone.1 | convolution fusion | flops 3284140032 | bytes 80805888 | tf_op jit(solution)/shard_map/while/body/eval_jaxpr/qhgd,khd->hgqk/dot_general | solution.py:48
  217.9 14.8 %fusion.138 = f32[8,128,2,512]{3,1,2,0:T(8,128)} fusion(bf16[1536,8,128,1]{0,2,3,1:T(8,128)(2,1)} %bitcast.150, bf16[8,2,512,1536]{2,3,1,0:T(8,128)(2,1)} %fusion.136), kind=kOutput, calls=%fused_computation.89.clone.1 | convolution fusion | flops 3221225472 | bytes 32505856 | tf_op jit(solution)/shard_map/while/body/eval_jaxpr/hgqk,khd->qhgd/dot_general | solution.py:52
  232.7 14.5 %fusion.137 = f32[8,128,1536,1]{2,1,3,0:T(8,128)} fusion(bf16[512,8,2,128]{0,3,2,1:T(8,128)(2,1)S(1)} %bitcast.152, bf16[8,2,512,1536]{2,3,1,0:T(8,128)(2,1)} %fusion.136), kind=kOutput, calls=%fused_computation.87.clone.1 | convolution fusion | flops 3221225472 | bytes 33554432 | tf_op jit(solution)/shard_map/while/body/eval_jaxpr/hgqk,qhgd->khd/dot_general | solution.py:55
  247.2 5.6 copy.71
  252.8 4.8 constant_dynamic-update-slice_fusion.6
  257.6 11.3 %constant_dynamic-update-slice_fusion.5 = (f32[2048,1024]{0,1:T(8,128)}, f32[2048,1024]{0,1:T(8,128)}) fusion(f32[2048,1024]{0,1:T(8,128)} %get-tuple-element.255, s32[]{:T(128)S(6)} %select_n.36, f32[8,128,1536,1]{2,1,3,0:T(8,128)S(1)} %bitcast.140, f32[2048,1024]{0,1:T(8,128)} %get-tuple-element.254, f32[8,128,1536,1]{2,1,3,0:T(8,128)} %fusion.137), kind=kLoop, calls=%fused_computation.24.clone.1 | loop fusion | flops 3145728 | bytes 37748740 | tf_op jit(solution)/shard_map/while/body/eval_jaxpr/dynamic_update_slice | solution.py:136
  302.3 24.5 %fusion.132 = (f32[8,2,512]{2,1,0:T(2,128)S(1)}, f32[8,2,512,1536]{2,3,1,0:T(8,128)}) fusion(pred[512,1536]{0,1:T(8,128)(4,1)S(1)} %fusion.131, bf16[1536,8,128,1]{0,2,3,1:T(8,128)(2,1)} %bitcast.149, bf16[512,8,2,128]{0,3,2,1:T(8,128)(2,1)} %bitcast.151), kind=kOutput, calls=%fused_computation.86.clone.1 | convolution fusion | flops 3271558656 | bytes 56393728 | tf_op jit(solution)/shard_map/while/body/eval_jaxpr/sub | solution.py:41
  326.8 27.4 %fusion.133 = bf16[8,2,512,1536]{2,3,1,0:T(8,128)(2,1)} fusion(f32[8,2,512,1536]{2,3,1,0:T(8,128)} %get-tuple-element.234, f32[8,2,512]{2,1,0:T(2,128)S(1)} %get-tuple-element.235), kind=kLoop, calls=%fused_computation.11.clone.1 | loop fusion | flops 25165824 | bytes 75530240 | tf_op jit(solution)/shard_map/while/body/eval_jaxpr/convert_element_type | solution.py:43
  354.2 12.6 %fusion.135 = f32[512,8,2]{0,2,1:T(2,128)S(1)} fusion(bf16[512,8,2,128]{0,3,2,1:T(8,128)(2,1)S(1)} %bitcast.141, bf16[1536,8,128,1]{0,2,3,1:T(8,128)(2,1)} %bitcast.147, bf16[8,2,512,1536]{2,3,1,0:T(8,128)(2,1)} %fusion.133), kind=kOutput, calls=%fused_computation.18.clone.1 | convolution fusion | flops 3224363008 | bytes 30441472 | tf_op jit(solution)/shard_map/while/body/eval_jaxpr/hgqk,khd->qhgd/dot_general | solution.py:44
  366.8 14.5 %fusion.134 = f32[8,128,1536,1]{2,1,3,0:T(8,128)} fusion(bf16[512,8,2,128]{0,3,2,1:T(8,128)(2,1)S(1)} %bitcast.142, bf16[8,2,512,1536]{2,3,1,0:T(8,128)(2,1)} %fusion.133), kind=kOutput, calls=%fused_computation.88.clone.1 | convolution fusion | flops 3221225472 | bytes 33554432 | tf_op jit(solution)/shard_map/while/body/eval_jaxpr/hgqk,qhgd->khd/dot_general | solution.py:58
  381.3 25.9 %fusion.136 = bf16[8,2,512,1536]{2,3,1,0:T(8,128)(2,1)} fusion(bf16[1536,8,128,1]{0,2,3,1:T(8,128)(2,1)} %bitcast.148, bf16[512,8,2,128]{0,3,2,1:T(8,128)(2,1)S(1)} %bitcast.143, f32[8,2,512]{2,1,0:T(2,128)S(1)} %bitcast.157, f32[8,2,512,1536]{2,3,1,0:T(8,128)} %get-tuple-element.234, f32[8,2,512]{2,1,0:T(2,128)S(1)} %get-tuple-element.235), kind=kOutput, calls=%fused_computation.3.clone.1 | convolution fusion | flops 3284140032 | bytes 80805888 | tf_op jit(solution)/shard_map/while/body/eval_jaxpr/qhgd,khd->hgqk/dot_general | solution.py:48
  407.2 14.8 %fusion.138 = f32[8,128,2,512]{3,1,2,0:T(8,128)} fusion(bf16[1536,8,128,1]{0,2,3,1:T(8,128)(2,1)} %bitcast.150, bf16[8,2,512,1536]{2,3,1,0:T(8,128)(2,1)} %fusion.136), kind=kOutput, calls=%fused_computation.89.clone.1 | convolution fusion | flops 3221225472 | bytes 32505856 | tf_op jit(solution)/shard_map/while/body/eval_jaxpr/hgqk,khd->qhgd/dot_general | solution.py:52
  422.0 14.5 %fusion.137 = f32[8,128,1536,1]{2,1,3,0:T(8,128)} fusion(bf16[512,8,2,128]{0,3,2,1:T(8,128)(2,1)S(1)} %bitcast.152, bf16[8,2,512,1536]{2,3,1,0:T(8,128)(2,1)} %fusion.136), kind=kOutput, calls=%fused_computation.87.clone.1 | convolution fusion | flops 3221225472 | bytes 33554432 | tf_op jit(solution)/shard_map/while/body/eval_jaxpr/hgqk,qhgd->khd/dot_general | solution.py:55
  436.5 5.6 copy.71
  442.1 4.8 constant_dynamic-update-slice_fusion.6
  446.9 11.2 %constant_dynamic-update-slice_fusion.5 = (f32[2048,1024]{0,1:T(8,128)}, f32[2048,1024]{0,1:T(8,128)}) fusion(f32[2048,1024]{0,1:T(8,128)} %get-tuple-element.255, s32[]{:T(128)S(6)} %select_n.36, f32[8,128,1536,1]{2,1,3,0:T(8,128)S(1)} %bitcast.140, f32[2048,1024]{0,1:T(8,128)} %get-tuple-element.254, f32[8,128,1536,1]{2,1,3,0:T(8,128)} %fusion.137), kind=kLoop, calls=%fused_computation.24.clone.1 | loop fusion | flops 3145728 | bytes 37748740 | tf_op jit(solution)/shard_map/while/body/eval_jaxpr/dynamic_update_slice | solution.py:136
  481.4 7.4 %convolution_multiply_fusion.3 = f32[16,2048]{1,0:T(8,128)} fusion(f32[1024,2048]{1,0:T(8,128)} %bitcast.155, f32[1024,48]{0,1:T(8,128)S(1)} %copy-done.6), kind=kOutput, calls=%fused_computation.60 | convolution fusion | flops 402685952 | bytes 8585216 | tf_op jit(solution)/shard_map/dot_general | solution.py:178
  488.8 5.8 fusion.16
  494.6 6.3 fusion.41
  505.4 25.7 %all-reduce.11.cloned.1.call-done = (f32[1024,48]{0,1:T(8,128)}, f32[1024,32]{0,1:T(8,128)}) async-done(((f32[1024,48]{0,1:T(8,128)}, f32[1024,32]{0,1:T(8,128)}), (f32[1024,48]{0,1:T(8,128)}, f32[1024,32]{0,1:T(8,128)})) %all-reduce.11.cloned.1.call-update) | async-done | bytes 327696 | tf_op jit(solution)/shard_map/psum | solution.py:167
  532.9 6.3 fusion.44
  540.2 7.6 %fusion.34 = f32[2688,16]{0,1:T(8,128)} fusion(bf16[2688,1024]{1,0:T(8,128)(2,1)} %param.13, f32[1024,48]{0,1:T(8,128)S(1)} %pad_add_fusion), kind=kOutput, calls=%fused_computation.59 | convolution fusion | flops 528525312 | bytes 5742592 | tf_op jit(solution)/shard_map/dot_general | solution.py:190
  547.8 5.0 fusion.33
  552.8 5.0 fusion.32
  557.9 95.0 %all-reduce.9.cloned.1.call-done = (f32[2688,16]{0,1:T(8,128)}, f32[16,2048]{1,0:T(8,128)}, f32[2688,16]{0,1:T(8,128)}, f32[16,1024]{1,0:T(8,128)}, f32[2688,16]{0,1:T(8,128)}, /*index=5*/f32[16,1024]{1,0:T(8,128)}) async-done(((f32[2688,16]{0,1:T(8,128)}, f32[16,2048]{1,0:T(8,128)}, f32[2688,16]{0,1:T(8,128)}, f32[16,1024]{1,0:T(8,128)}, f32[2688,16]{0,1:T(8,128)}, /*index=5*/f32[16,1024]{1,0:T(8,128)}), ...) | async-done | bytes 778256 | tf_op jit(solution)/shard_map/psum | solution.py:193
  (107 shorter events, 137.8 us)
Async XLA Ops:
  7.2 47.3 %copy-start = (bf16[16,2048]{1,0:T(8,128)(2,1)S(1)}, bf16[16,2048]{1,0:T(8,128)(2,1)}, u32[]{:S(2)}) copy-start(bf16[16,2048]{1,0:T(8,128)(2,1)} %param.19) | copy-start | bytes 196612
  7.2 30.0 %copy-start.7 = (bf16[16,1024]{1,0:T(8,128)(2,1)S(1)}, bf16[16,1024]{1,0:T(8,128)(2,1)}, u32[]{:S(2)}) copy-start(bf16[16,1024]{1,0:T(8,128)(2,1)} %param.21) | copy-start | bytes 98308
  7.2 30.0 %copy-start.4 = (bf16[1024,1024]{1,0:T(8,128)(2,1)S(1)}, bf16[1024,1024]{1,0:T(8,128)(2,1)}, u32[]{:S(2)}) copy-start(bf16[1024,1024]{1,0:T(8,128)(2,1)} %param.15) | copy-start | bytes 6291460
  7.2 36.8 %copy-start.9 = (bf16[16,1024]{1,0:T(8,128)(2,1)S(1)}, bf16[16,1024]{1,0:T(8,128)(2,1)}, u32[]{:S(2)}) copy-start(bf16[16,1024]{1,0:T(8,128)(2,1)} %param.23) | copy-start | bytes 98308
  7.2 29.9 %all-reduce.7.cloned.1.call-start = ((), (), s32[]{:S(2)}) async-start(), calls=%async_computation | async-start | bytes 393216 | tf_op jit(solution)/shard_map/psum | solution.py:106
  11.9 519.3 %all-reduce.11.cloned.1.call-start = ((), (), s32[]{:S(2)}) async-start(), calls=%async_computation.2 | async-start | bytes 655360 | tf_op jit(solution)/shard_map/psum | solution.py:167
  37.2 14.7 %copy-start.5 = (f32[1024,48]{0,1:T(8,128)S(1)}, f32[1024,48]{0,1:T(8,128)}, u32[]{:S(2)}) copy-start(f32[1024,48]{0,1:T(8,128)} %all-reduce.7.cloned.1.call-done) | copy-start | bytes 589828
  41.4 20.1 %collective-permute-start = (bf16[1024,1024]{1,0:T(8,128)(2,1)}, bf16[1024,1024]{1,0:T(8,128)(2,1)}, u32[]{:S(2)}, u32[]{:S(2)}) collective-permute-start(bf16[1024,1024]{1,0:T(8,128)(2,1)} %add_convert_fusion.2), channel_id=1, source_target_pairs={{0,2},{2,4},{4,6},{6,8},{8,10},{10,12},{12,14},{14,16},{16,18},{18... | collective-permute-start | bytes 6291464 | tf_op jit(solution)/shard_map/ppermute | solution.py:17
  47.7 18.5 %collective-permute-start.1 = (bf16[1024,1024]{1,0:T(8,128)(2,1)S(1)}, bf16[1024,1024]{1,0:T(8,128)(2,1)}, u32[]{:S(2)}, u32[]{:S(2)}) collective-permute-start(bf16[1024,1024]{1,0:T(8,128)(2,1)S(1)} %add_convert_fusion.1), channel_id=1, source_target_pairs={{0,2},{2,4},{4,6},{6,8},{8,10},{10,12},{12,14},{14,16},{16,18},{18... | collective-permute-start | bytes 6291464 | tf_op jit(solution)/shard_map/ppermute | solution.py:17
  52.5 436.2 %collective-permute-start.3 = (f32[1024,32]{0,1:T(8,128)}, f32[1024,32]{0,1:T(8,128)}, u32[]{:S(2)}, u32[]{:S(2)}) collective-permute-start(f32[1024,32]{0,1:T(8,128)} %slice.57), channel_id=1, source_target_pairs={{0,2},{2,4},{4,6},{6,8},{8,10},{10,12},{12,14},{14,16},{16,18},{18... | collective-permute-start | bytes 393224 | tf_op jit(solution)/shard_map/ppermute | solution.py:17
  79.4 385.9 %copy-start.8 = (bf16[16,1024]{1,0:T(8,128)(2,1)S(1)}, bf16[16,1024]{1,0:T(8,128)(2,1)}, u32[]{:S(2)}) copy-start(bf16[16,1024]{1,0:T(8,128)(2,1)} %param.21) | copy-start | bytes 98308
  217.9 14.8 %copy-start.2 = (bf16[512,2048]{0,1:T(8,128)(2,1)S(1)}, bf16[512,2048]{0,1:T(8,128)(2,1)}, u32[]{:S(2)}) copy-start(bf16[512,2048]{0,1:T(8,128)(2,1)} %copy.69) | copy-start | bytes 6291460 | tf_op jit(solution)/shard_map/while
  247.2 10.4 %slice-start = ((s8[6291456]{0:T(1024)(128)(4,1)}), s8[2097152]{0:T(1024)(128)(4,1)S(1)}, s32[]{:S(2)}) async-start(s8[6291456]{0:T(1024)(128)(4,1)} %bitcast.139), calls=%async_computation.3 | async-start | bytes 4194304 | tf_op jit(solution)/shard_map/while
  252.8 4.8 slice-start.1
  407.2 14.8 %copy-start.2 = (bf16[512,2048]{0,1:T(8,128)(2,1)S(1)}, bf16[512,2048]{0,1:T(8,128)(2,1)}, u32[]{:S(2)}) copy-start(bf16[512,2048]{0,1:T(8,128)(2,1)} %copy.69) | copy-start | bytes 6291460 | tf_op jit(solution)/shard_map/while
  436.5 10.4 %slice-start = ((s8[6291456]{0:T(1024)(128)(4,1)}), s8[2097152]{0:T(1024)(128)(4,1)S(1)}, s32[]{:S(2)}) async-start(s8[6291456]{0:T(1024)(128)(4,1)} %bitcast.139), calls=%async_computation.3 | async-start | bytes 4194304 | tf_op jit(solution)/shard_map/while
  442.1 4.8 slice-start.1
  465.3 7.6 %copy-start.1 = (f32[2048,1024]{0,1:T(8,128)S(1)}, f32[2048,1024]{0,1:T(8,128)}, u32[]{:S(2)}) copy-start(f32[2048,1024]{0,1:T(8,128)} %get-tuple-element.126) | copy-start | bytes 25165828
  465.3 7.6 %copy-start.10 = (bf16[16,1024]{1,0:T(8,128)(2,1)S(1)}, bf16[16,1024]{1,0:T(8,128)(2,1)}, u32[]{:S(2)}) copy-start(bf16[16,1024]{1,0:T(8,128)(2,1)} %param.23) | copy-start | bytes 98308
  469.1 6.8 %copy-start.3 = (f32[2,512,2048]{2,1,0:T(8,128)S(1)}, f32[2,512,2048]{2,1,0:T(8,128)}, u32[]{:S(2)}) copy-start(f32[2,512,2048]{2,1,0:T(8,128)} %get-tuple-element.124) | copy-start | bytes 25165828
  475.9 5.5 copy-start.6
  481.3 171.6 %all-reduce.9.cloned.1.call-start = ((), (), s32[]{:S(2)}) async-start(), calls=%async_computation.1 | async-start | bytes 1556480 | tf_op jit(solution)/shard_map/psum | solution.py:193
  481.3 19.6 %slice-start.2 = ((s8[8388608]{0:T(1024)(128)(4,1)}), s8[4194304]{0:T(1024)(128)(4,1)S(1)}, s32[]{:S(2)}) async-start(s8[8388608]{0:T(1024)(128)(4,1)} %bitcast.145), calls=%async_computation.5 | async-start | bytes 8388608
  488.7 12.2 %slice-start.3 = ((s8[8388608]{0:T(1024)(128)(4,1)}), s8[4194304]{0:T(1024)(128)(4,1)S(1)}, s32[]{:S(2)}) async-start(s8[8388608]{0:T(1024)(128)(4,1)} %bitcast.145), calls=%async_computation.6 | async-start | bytes 8388608
  500.9 46.9 %slice-start.4 = ((s8[5505024]{0:T(1024)(128)(4,1)}), s8[1310720]{0:T(1024)(128)(4,1)S(1)}, s32[]{:S(2)}) async-start(s8[5505024]{0:T(1024)(128)(4,1)} %bitcast.153), calls=%async_computation.7 | async-start | bytes 2621440
  531.1 16.7 %slice-start.5 = ((s8[5505024]{0:T(1024)(128)(4,1)}), s8[4194304]{0:T(1024)(128)(4,1)S(1)}, s32[]{:S(2)}) async-start(s8[5505024]{0:T(1024)(128)(4,1)} %bitcast.153), calls=%async_computation.8 | async-start | bytes 8388608
  531.1 8.1 %collective-permute-start.2 = (f32[1024,32]{0,1:T(8,128)}, f32[1024,32]{0,1:T(8,128)S(1)}, u32[]{:S(2)}, u32[]{:S(2)}) collective-permute-start(f32[1024,32]{0,1:T(8,128)} %get-tuple-element.164), channel_id=1, source_target_pairs={{2,0},{4,2},{6,4},{8,6},{10,8},{12,10},{14,12},{16,14},{18,16},{20... | collective-permute-start | bytes 393224 | tf_op jit(solution)/shard_map/ppermute | solution.py:17
Sparse Core Ops, SparseCore 0:
  12.0 25.1 all-reduce.6
  481.4 49.6 all-reduce.10
  558.0 94.8 all-reduce.8
where the time goes:
time: 678 us; the launch traced here: 669 us
  matrix products  296 us (44%)
  waiting for transfers between devices  146 us (22%)
  local copies, waits for them, and re-layouts  103 us (15%)
  other arithmetic  91 us (13%)
  between operations  14.3 us (2%)
  starting transfers between devices  10.6 us (2%)
  loops' own time  8.82 us (1%)
    psum x1, waiting for transfers between devices, on_device(): lax.psum((query_down_gradient, query_up_gradient, key_down_gradient, key_...  95 us
    convert_element_type x2, other arithmetic, band_grad(): weights_low = weights.astype(jnp.bfloat16)  54.9 us
    dot_general x2, matrix products, band_grad(): jnp.einsum('qhgd,khd->hgqk', grad_heads, value_heads, preferred_element_t...  51.8 us
    sub x2, matrix products, band_grad(): exponent = jnp.exp(scores - highest_score)  49 us
    dot_general x2, matrix products, band_grad(): jnp.einsum('hgqk,khd->qhgd', grad_low, key_heads, preferred_element_type=...  29.5 us
    dot_general x2, matrix products, band_grad(): jnp.einsum('hgqk,qhgd->khd', grad_low, query_heads, preferred_element_typ...  29 us
    dot_general x2, matrix products, band_grad(): jnp.einsum('hgqk,qhgd->khd', weights_low, grad_heads, preferred_element_t...  28.9 us
    psum x1, waiting for transfers between devices, on_device(): lax.psum((partial_inner, partial_prior), 'heads')  25.7 us
  transfers between devices with their start and end apart: 7, of which 3 were waited for; matrix products, arithmetic and copies ran while one was open for 68% of the time, Pallas kernels for 0%

commit v1 on v0

v1 whole, which is shorter than its diff:
```python
import functools

import jax
import jax.numpy as jnp
from jax import lax
from jax.experimental import pallas as pl
from jax.experimental.pallas import tpu as pltpu
from jax.sharding import PartitionSpec as P

HEAD_WIDTH = 128
WINDOW = 1024
ADAPTER_SCALE = 2.0
NEGATIVE = -1e30
LOG2E = 1.4426950408889634
F32 = jnp.float32
BF16 = jnp.bfloat16


def split2(x):
    high = x.astype(BF16)
    return high, (x - high.astype(F32)).astype(BF16)


def split3(x):
    high = x.astype(BF16)
    rest = x - high.astype(F32)
    middle = rest.astype(BF16)
    return high, middle, (rest - middle.astype(F32)).astype(BF16)


def dot_nn(a, b):
    return lax.dot_general(a, b, (((1,), (0,)), ((), ())), preferred_element_type=F32)


def dot_nt(a, b):
    return lax.dot_general(a, b, (((1,), (1,)), ((), ())), preferred_element_type=F32)


def fold8(x, reduce):
    return reduce(x.reshape(x.shape[0] // 8, 8, x.shape[1]), axis=0)


def attention_body(
    group,
    rank,
    bias_ref,
    rank_ref,
    prior_rank_ref,
    fq_ref,
    do_ref,
    fk_ref,
    pk_ref,
    fv_ref,
    pv_ref,
    uq_ref,
    uk_ref,
    uv_ref,
    inner_ref,
    inner_prior_ref,
    upq_ref,
    upk_ref,
    upv_ref,
    ranks_t,
    ranks,
    k_all,
    v_all,
    k_t,
    dk_acc,
    dv_acc,
    s_scr,
    dp_scr,
):
    head = pl.program_id(0)
    block = pl.program_id(1)
    rows = fq_ref.shape[0]
    own = fk_ref.shape[0]
    width = HEAD_WIDTH
    tiles = own // rows
    scale = width**-0.5
    factor = scale * LOG2E

    @pl.when((head == 0) & (block == 0))
    def _():
        mine = split3(rank_ref[...])
        prior = split3(prior_rank_ref[...])
        blank = jnp.zeros((rank, own), BF16)
        for part in range(3):
            at = part * 3 * rank
            ranks_t[at : at + 3 * rank, own:] = mine[part]
            ranks_t[at : at + rank, :own] = blank
            ranks_t[at + rank : at + 3 * rank, :own] = prior[part]
        ranks[...] = ranks_t[...].astype(F32).T.astype(BF16)
        inner_ref[...] = jnp.zeros_like(inner_ref)
        inner_prior_ref[...] = jnp.zeros_like(inner_prior_ref)

    def stacked(up, kind):
        pieces = []
        for _ in range(3):
            for other in range(3):
                pieces.append(up if other == kind else jnp.zeros_like(up))
        return jnp.concatenate(pieces, axis=0)

    def rank_rows(kind, start, size):
        pieces = [
            ranks_t[(3 * part + kind) * rank : (3 * part + kind + 1) * rank, pl.ds(start, size)]
            for part in range(3)
        ]
        return jnp.concatenate(pieces, axis=0)

    def merged(x):
        return x[:rank] + x[rank : 2 * rank] + x[2 * rank :]

    def lifted(base, rank_part, up):
        return (base.astype(F32) + ADAPTER_SCALE * dot_nn(rank_part, up)).astype(BF16)

    @pl.when(block == 0)
    def _():
        up_k = stacked(uk_ref[...], 1)
        up_v = stacked(uv_ref[...], 2)
        k_all[:own] = lifted(pk_ref[...], ranks[:own], up_k)
        k_all[own:] = lifted(fk_ref[...], ranks[own:], up_k)
        v_all[:own] = lifted(pv_ref[...], ranks[:own], up_v)
        v_all[own:] = lifted(fv_ref[...], ranks[own:], up_v)
        k_t[...] = k_all[...].T
        dk_acc[...] = jnp.zeros_like(dk_acc)
        dv_acc[...] = jnp.zeros_like(dv_acc)
        upq_ref[...] = jnp.zeros_like(upq_ref)

    base = pl.multiple_of(block * rows, rows)

    def at(tile):
        return pl.multiple_of(base + tile * rows, rows)

    rank_part = ranks[pl.ds(at(tiles), rows), :]
    q = lifted(fq_ref[...], rank_part, stacked(uq_ref[...], 0))
    q_cat = jnp.concatenate([q[:, g * width : (g + 1) * width] for g in range(group)], axis=0)
    do = do_ref[...]
    do_t = jnp.concatenate([do[:, g * width : (g + 1) * width].T for g in range(group)], axis=1)
    key_at = lax.broadcasted_iota(jnp.int32, (rows, rows), 0)
    query_at = lax.broadcasted_iota(jnp.int32, (rows, rows), 1)
    earlier = jnp.concatenate([key_at > query_at] * group, axis=1)
    bias = bias_ref[0]

    biases = []
    highest = None
    for tile in range(tiles):
        tile_bias = jnp.where(block + tile < tiles, bias, 0.0)
        scores = dot_nt(k_all[pl.ds(at(tile), rows), :], q_cat)
        grads = dot_nn(v_all[pl.ds(at(tile), rows), :], do_t)
        if tile == 0:
            last = dot_nt(k_all[pl.ds(at(tiles), rows), :], q_cat)
            scores = jnp.where(earlier, scores + bias, last)
            grads = jnp.where(earlier, grads, dot_nn(v_all[pl.ds(at(tiles), rows), :], do_t))
            tile_bias = jnp.float32(0.0)
        biases.append(tile_bias)
        s_scr[tile] = scores
        dp_scr[tile] = grads
        high = fold8(scores, jnp.max) + tile_bias
        highest = high if highest is None else jnp.maximum(highest, high)
    top = jnp.max(highest, axis=0, keepdims=True) * factor
    total = jnp.zeros((8, group * rows), F32)
    dots = jnp.zeros((8, group * rows), F32)
    for tile in range(tiles):
        exponent = jnp.exp2(s_scr[tile] * factor - (top - biases[tile]))
        s_scr[tile] = exponent
        total = total + fold8(exponent, jnp.sum)
        dots = dots + fold8(exponent * dp_scr[tile], jnp.sum)
    inverse = 1.0 / jnp.sum(total, axis=0, keepdims=True)
    row_dots = jnp.sum(dots, axis=0, keepdims=True) * inverse
    do_scaled = (do_t.astype(F32) * inverse).astype(BF16)
    column = jnp.broadcast_to(inverse, (8, group * rows)).T[:, :1]
    q_scaled = (q_cat.astype(F32) * column).astype(BF16)
    dq_t = jnp.zeros((width, group * rows), F32)

    def spread(tile, grad_low, weight_low):
        dk_acc[pl.ds(at(tile), rows), :] += dot_nn(grad_low, q_scaled)
        dv_acc[pl.ds(at(tile), rows), :] += dot_nt(weight_low, do_scaled)
        return dot_nn(k_t[:, pl.ds(at(tile), rows)], grad_low)

    for tile in range(tiles):
        exponent = s_scr[tile]
        grad = exponent * (dp_scr[tile] - row_dots)
        if tile == 0:
            zero = jnp.zeros_like(grad)
            dq_t = dq_t + spread(
                0,
                jnp.where(earlier, grad, zero).astype(BF16),
                jnp.where(earlier, exponent, zero).astype(BF16),
            )
            dq_t = dq_t + spread(
                tiles,
                jnp.where(earlier, zero, grad).astype(BF16),
                jnp.where(earlier, zero, exponent).astype(BF16),
            )
        else:
            dq_t = dq_t + spread(tile, grad.astype(BF16), exponent.astype(BF16))

    dq = dq_t * (inverse * scale)
    up_q = uq_ref[...]
    rank_q = rank_rows(0, at(tiles), rows)
    for part in split2(dq):
        tall = jnp.concatenate([part[:, g * rows : (g + 1) * rows] for g in range(group)], axis=0)
        inner_ref[:rank, pl.ds(base, rows)] += dot_nn(up_q, tall)
        upq_ref[...] += merged(dot_nt(rank_q, tall))

    @pl.when(block == tiles - 1)
    def _():
        for kind, acc, up_ref, out_ref, mult in (
            (1, dk_acc, uk_ref, upk_ref, scale),
            (2, dv_acc, uv_ref, upv_ref, 1.0),
        ):
            rank_part = rank_rows(kind, 0, 2 * own)
            high, low = split2(acc[...] * mult)
            out_ref[...] = merged(dot_nn(rank_part, high) + dot_nn(rank_part, low))
            inner = dot_nt(up_ref[...], high) + dot_nt(up_ref[...], low)
            inner_prior_ref[(kind - 1) * rank : kind * rank, :] += inner[:, :own]
            inner_ref[kind * rank : (kind + 1) * rank, :] += inner[:, own:]


def attention(first, heads, bias, rank_t, prior_rank_t, fq, do, fk, pk, fv, pv, uq, uk, uv, rows=256):
    rank = uq.shape[0]
    own = fk.shape[0]
    width = HEAD_WIDTH
    group = fq.shape[1] // fk.shape[1]
    wide = group * width
    tiles = own // rows
    whole = lambda h, b: (0, 0)
    query = lambda h, b: (b, first + h)
    key = lambda h, b: (0, first + h)
    chunk = lambda h, b: (0, h)
    in_specs = [
        pl.BlockSpec(memory_space=pltpu.SMEM),
        pl.BlockSpec(rank_t.shape, whole),
        pl.BlockSpec(prior_rank_t.shape, whole),
        pl.BlockSpec((rows, wide), query),
        pl.BlockSpec((rows, wide), query),
        pl.BlockSpec((own, width), key),
        pl.BlockSpec((own, width), chunk),
        pl.BlockSpec((own, width), key),
        pl.BlockSpec((own, width), chunk),
        pl.BlockSpec((rank, wide), key),
        pl.BlockSpec((rank, width), key),
        pl.BlockSpec((rank, width), key),
    ]
    out_specs = [
        pl.BlockSpec((3 * rank, own), whole),
        pl.BlockSpec((2 * rank, own), whole),
        pl.BlockSpec((rank, wide), chunk),
        pl.BlockSpec((rank, width), chunk),
        pl.BlockSpec((rank, width), chunk),
    ]
    out_shape = [
        jax.ShapeDtypeStruct((3 * rank, own), F32),
        jax.ShapeDtypeStruct((2 * rank, own), F32),
        jax.ShapeDtypeStruct((rank, heads * wide), F32),
        jax.ShapeDtypeStruct((rank, heads * width), F32),
        jax.ShapeDtypeStruct((rank, heads * width), F32),
    ]
    scratch = [
        pltpu.VMEM((9 * rank, 2 * own), BF16),
        pltpu.VMEM((2 * own, 9 * rank), BF16),
        pltpu.VMEM((2 * own, width), BF16),
        pltpu.VMEM((2 * own, width), BF16),
        pltpu.VMEM((width, 2 * own), BF16),
        pltpu.VMEM((2 * own, width), F32),
        pltpu.VMEM((2 * own, width), F32),
        pltpu.VMEM((tiles, rows, group * rows), F32),
        pltpu.VMEM((tiles, rows, group * rows), F32),
    ]
    pairs = heads * group * own * own
    return pl.pallas_call(
        functools.partial(attention_body, group, rank),
        grid=(heads, tiles),
        in_specs=in_specs,
        out_specs=out_specs,
        out_shape=out_shape,
        scratch_shapes=scratch,
        compiler_params=pltpu.CompilerParams(
            dimension_semantics=("arbitrary", "arbitrary"), vmem_limit_bytes=48 * 2**20
        ),
        cost_estimate=pl.CostEstimate(
            flops=10 * pairs * width,
            transcendentals=pairs,
            bytes_accessed=heads * own * width * (4 * group + 8),
        ),
        name="banded_attention",
    )(bias, rank_t, prior_rank_t, fq, do, fk, pk, fv, pv, uq, uk, uv)


def shifted(shard, axis, by):
    length = lax.axis_size(axis)
    pairs = [(i, i + by) for i in range(length) if 0 <= i + by < length]
    return lax.ppermute(shard, axis, pairs)


def summed(shard, axis):
    length = lax.axis_size(axis)
    if length & (length - 1):
        return lax.psum(shard, axis)
    step = 1
    while step < length:
        pairs = [(i, i ^ step) for i in range(length)]
        shard = shard + lax.ppermute(shard, axis, pairs)
        step *= 2
    return shard


def reduced(shard, axis):
    length = lax.axis_size(axis)
    if length & (length - 1):
        return lax.psum(shard, axis)
    index = lax.axis_index(axis)
    step = 1
    while step < length:
        pairs = [(i, i ^ step) for i in range(length)]
        half = shard.shape[1] // 2
        first, second = shard[:, :half], shard[:, half:]
        low = (index // step) % 2 == 0
        kept = jnp.where(low, first, second)
        sent = jnp.where(low, second, first)
        shard = kept + lax.ppermute(sent, axis, pairs)
        step *= 2
    while step > 1:
        step //= 2
        pairs = [(i, i ^ step) for i in range(length)]
        low = (index // step) % 2 == 0
        other = lax.ppermute(shard, axis, pairs)
        first, second = jnp.where(low, shard, other), jnp.where(low, other, shard)
        shard = jnp.concatenate([first, second], axis=1)
    return shard


def on_device(
    activations,
    frozen_query_rows,
    frozen_key_rows,
    frozen_value_rows,
    output_gradient,
    query_down_weight,
    query_up_weight,
    key_down_weight,
    key_up_weight,
    value_down_weight,
    value_up_weight,
):
    rank = query_down_weight.shape[1]
    features = activations.shape[0]
    heads = frozen_key_rows.shape[1] // HEAD_WIDTH
    per_call = max(1, heads // 4)
    prior = []
    for first in range(0, heads, per_call):
        columns = slice(first * HEAD_WIDTH, (first + per_call) * HEAD_WIDTH)
        prior.append(
            shifted((frozen_key_rows[:, columns], frozen_value_rows[:, columns]), "ctx", 1)
        )
    down = jnp.concatenate([query_down_weight, key_down_weight, value_down_weight], axis=1)
    partial_rank = lax.dot_general(
        down, activations, (((0,), (0,)), ((), ())), preferred_element_type=F32
    )
    rank_t = summed(partial_rank, "heads")
    prior_rank_t = shifted(rank_t[rank:], "ctx", 1)
    bias = jnp.where(lax.axis_index("ctx") == 0, NEGATIVE, 0.0).astype(F32).reshape(1)
    inner = inner_prior = None
    ups = []
    for index, first in enumerate(range(0, heads, per_call)):
        prior_keys, prior_values = prior[index]
        one, one_prior, upq, upk, upv = attention(
            first,
            per_call,
            bias,
            rank_t,
            prior_rank_t,
            frozen_query_rows,
            output_gradient,
            frozen_key_rows,
            prior_keys,
            frozen_value_rows,
            prior_values,
            query_up_weight,
            key_up_weight,
            value_up_weight,
        )
        inner = one if inner is None else inner + one
        inner_prior = one_prior if inner_prior is None else inner_prior + one_prior
        ups.append((upq, upk, upv))
    back = shifted(inner_prior, "ctx", -1)
    inner = jnp.concatenate([inner[:rank], inner[rank:] + back], axis=0)
    inner = summed(inner, "heads")
    high, middle, low = split3(inner)
    parts = jnp.concatenate([high, middle, low], axis=0)
    down_parts = lax.dot_general(
        parts, activations, (((1,), (1,)), ((), ())), preferred_element_type=F32
    )
    down_t = down_parts[: 3 * rank] + down_parts[3 * rank : 6 * rank] + down_parts[6 * rank :]
    pieces = [down_t[kind * rank : (kind + 1) * rank] for kind in range(3)]
    pieces += [jnp.concatenate([up[kind] for up in ups], axis=1) for kind in range(3)]
    packed = ADAPTER_SCALE * jnp.concatenate(pieces, axis=1)
    unit = 128 * lax.axis_size("ctx")
    packed = jnp.pad(packed, ((0, 0), (0, -packed.shape[1] % unit)))
    packed = reduced(packed, "ctx")
    results = []
    start = 0
    for piece in pieces:
        results.append(packed[:, start : start + piece.shape[1]])
        start += piece.shape[1]
    dq, dk, dv, upq, upk, upv = results
    return dq.T, upq, dk.T, upk, dv.T, upv


def solution(mesh):
    in_specs = (
        P("heads", "ctx"),
        P("ctx", "heads"),
        P("ctx", "heads"),
        P("ctx", "heads"),
        P("ctx", "heads"),
        P("heads", None),
        P(None, "heads"),
        P("heads", None),
        P(None, "heads"),
        P("heads", None),
        P(None, "heads"),
    )
    out_specs = (
        P("heads", None),
        P(None, "heads"),
        P("heads", None),
        P(None, "heads"),
        P("heads", None),
        P(None, "heads"),
    )
    return jax.shard_map(
        on_device, mesh=mesh, in_specs=in_specs, out_specs=out_specs, check_vma=False
    )
```

time: 678 us -> 219 us (0.32); the launches traced: 669 us -> 219 us
  matrix products: 296 us -> 5.56 us
  Pallas kernels: 0 us -> 116 us
  waiting for transfers between devices: 146 us -> 38.3 us
  local copies, waits for them, and re-layouts: 103 us -> 11.3 us
  other arithmetic: 91 us -> 1.48 us
  starting transfers between devices: 10.6 us -> 44.4 us
  between operations: 14.3 us -> 1.23 us
  loops' own time: 8.82 us -> 0 us
    dot_general x27 -> x2, matrix products: 247 us -> 5.56 us  [the longest x1 4.48 us: on_device(): lax.dot_general(parts, activations, (((1,), (1,)), ((), ())), preferred_e...]
    psum x3 -> x0, waiting for transfers between devices: 146 us -> none  [the longest x1 95 us: on_device(): lax.psum((query_down_gradient, query_up_gradient, key_down_gradient, key_...]
    pallas_call x0 -> x4, Pallas kernels: none -> 116 us  [attention(): pl.pallas_call(functools.partial(attention_body, group, rank), grid=(head...]
    dynamic_slice x18 -> x0, local copies, waits for them, and re-layouts: 62.8 us -> none  [the longest x4 17.1 us: advance(): lax.dynamic_slice_in_dim(span_values, offset, block_rows + window, 0)]
    convert_element_type x2 -> x1, other arithmetic: 54.9 us -> 0.04 us  [split3(): high = x.astype(BF16)]
    sub x2 -> x0, matrix products: 49 us -> none  [band_grad(): exponent = jnp.exp(scores - highest_score)]
    ppermute x0 -> x10, waiting for transfers between devices: none -> 35.3 us  [the longest x4 13 us: reduced(): shard = kept + lax.ppermute(sent, axis, pairs)]
    dynamic_update_slice x2 -> x0, other arithmetic: 22.6 us -> none  [advance(): lax.dynamic_update_slice_in_dim(sum_values, lax.dynamic_slice_in_dim(sum_...]
  transfers between devices with their start and end apart: 7 -> 20, of which waited for: 3 -> 11; matrix products, arithmetic and copies ran while one was open for 68% -> 1% of each run, Pallas kernels for 0% -> 40%
where the time goes in v1:
time: 219 us
  Pallas kernels  116 us (53%)
  starting transfers between devices  44.4 us (20%)
  waiting for transfers between devices  38.3 us (17%)
  local copies, waits for them, and re-layouts  11.3 us (5%)
  matrix products  5.56 us (3%)
    pallas_call x4, Pallas kernels, attention(): pl.pallas_call(functools.partial(attention_body, group, rank), grid=(head...  116 us
    ppermute x10, starting transfers between devices, shifted(): return lax.ppermute(shard, axis, pairs)  27 us
    ppermute x4, waiting for transfers between devices, reduced(): shard = kept + lax.ppermute(sent, axis, pairs)  13 us
    ppermute x4, waiting for transfers between devices, reduced(): other = lax.ppermute(shard, axis, pairs)  12.8 us
    ppermute x4, starting transfers between devices, reduced(): shard = kept + lax.ppermute(sent, axis, pairs)  9.79 us
    ppermute x2, waiting for transfers between devices, summed(): shard = shard + lax.ppermute(shard, axis, pairs)  9.48 us
    unnamed x44, local copies, waits for them, and re-layouts  4.88 us
    ppermute x4, starting transfers between devices, reduced(): other = lax.ppermute(shard, axis, pairs)  4.53 us
  transfers between devices with their start and end apart: 20, of which 11 were waited for; matrix products, arithmetic and copies ran while one was open for 1% of the time, Pallas kernels for 40%

profile of v1, /device:TPU:0, one launch (start us, length us, event | category | flops | bytes accessed | tf_op | source)
XLA Modules:
  0.0 218.5 jit_solution(16693414644371697250)
XLA Ops:
  0.7 3.0 %fusion.17 = (bf16[1024,256]{1,0:T(8,128)(2,1)}, bf16[1024,256]{1,0:T(8,128)(2,1)}, bf16[1024,256]{1,0:T(8,128)(2,1)}, bf16[1024,256]{1,0:T(8,128)(2,1)}) fusion(bf16[1024,1024]{1,0:T(8,128)(2,1)} %fk_ref.7), kind=kLoop, calls=%fused_computation.65 | loop fusion | bytes 4194304 | tf_op jit(solution)/shard_map/slice | solution.py:354
  3.7 2.5 %collective-permute-start.2 = (bf16[1024,256]{1,0:T(8,128)(2,1)}, bf16[1024,256]{1,0:T(8,128)(2,1)S(1)}, u32[]{:S(2)}, u32[]{:S(2)}) collective-permute-start(bf16[1024,256]{1,0:T(8,128)(2,1)} %get-tuple-element.52), channel_id=1, source_target_pairs={{0,2},{2,4},{4,6},{6,8},{8,10},{10,12},{12,14},{14,16},{16,18},{18... | collective-permute-start | bytes 1572872 | tf_op jit(solution)/shard_map/ppermute | solution.py:293
  7.7 4.6 %collective-permute-start.3 = (bf16[1024,256]{1,0:T(8,128)(2,1)}, bf16[1024,256]{1,0:T(8,128)(2,1)S(1)}, u32[]{:S(2)}, u32[]{:S(2)}) collective-permute-start(bf16[1024,256]{1,0:T(8,128)(2,1)} %get-tuple-element.48), channel_id=1, source_target_pairs={{0,2},{2,4},{4,6},{6,8},{8,10},{10,12},{12,14},{14,16},{16,18},{18... | collective-permute-start | bytes 1572872 | tf_op jit(solution)/shard_map/ppermute | solution.py:293
  13.5 1.6 collective-permute-start
  15.0 5.3 %collective-permute-done = f32[48,1024]{1,0:T(8,128)S(1)} collective-permute-done((f32[48,1024]{1,0:T(8,128)S(1)}, f32[48,1024]{1,0:T(8,128)S(1)}, u32[]{:S(2)}, u32[]{:S(2)}) %collective-permute-start) | collective-permute-done | bytes 196640 | tf_op jit(solution)/shard_map/ppermute | solution.py:303
  22.3 5.0 %collective-permute-start.4 = (bf16[1024,256]{1,0:T(8,128)(2,1)}, bf16[1024,256]{1,0:T(8,128)(2,1)}, u32[]{:S(2)}, u32[]{:S(2)}) collective-permute-start(bf16[1024,256]{1,0:T(8,128)(2,1)} %get-tuple-element.50), channel_id=1, source_target_pairs={{0,2},{2,4},{4,6},{6,8},{8,10},{10,12},{12,14},{14,16},{16,18},{18... | collective-permute-start | bytes 1572872 | tf_op jit(solution)/shard_map/ppermute | solution.py:293
  27.3 2.1 collective-permute-start.5
  30.1 2.6 %collective-permute-start.6 = (bf16[1024,256]{1,0:T(8,128)(2,1)}, bf16[1024,256]{1,0:T(8,128)(2,1)S(1)}, u32[]{:S(2)}, u32[]{:S(2)}) collective-permute-start(bf16[1024,256]{1,0:T(8,128)(2,1)} %get-tuple-element.51), channel_id=1, source_target_pairs={{0,2},{2,4},{4,6},{6,8},{8,10},{10,12},{12,14},{14,16},{16,18},{18... | collective-permute-start | bytes 1572872 | tf_op jit(solution)/shard_map/ppermute | solution.py:293
  32.6 1.9 collective-permute-start.7
  34.6 3.5 %collective-permute-start.8 = (bf16[1024,256]{1,0:T(8,128)(2,1)}, bf16[1024,256]{1,0:T(8,128)(2,1)S(1)}, u32[]{:S(2)}, u32[]{:S(2)}) collective-permute-start(bf16[1024,256]{1,0:T(8,128)(2,1)} %get-tuple-element.53), channel_id=1, source_target_pairs={{0,2},{2,4},{4,6},{6,8},{8,10},{10,12},{12,14},{14,16},{16,18},{18... | collective-permute-start | bytes 1572872 | tf_op jit(solution)/shard_map/ppermute | solution.py:293
  38.2 1.6 copy-done.2
  42.2 29.0 %banded_attention.4 = (f32[48,1024]{1,0:T(8,128)S(1)}, f32[32,1024]{1,0:T(8,128)S(1)}, f32[16,512]{1,0:T(8,128)S(1)}, f32[16,256]{1,0:T(8,128)S(1)}, f32[16,256]{1,0:T(8,128)S(1)}) custom-call(f32[1]{0:T(128)} %bitcast.bias_ref, f32[48,1024]{1,0:T(8,128)S(1)} %add.72.rank_ref, f32[32,1024]{1,0:T(8,128)S(1)} %copy-done.4, bf16[1024,2048]{1,0:T(8,128)(2,1)} %fq_ref.7, ...), custom_call_target="tpu_custom_call" | custom-call | flops 5368709120 | bytes 4194304 | tf_op jit(solution)/shard_map/banded_attention/pallas_call | solution.py:271
  71.3 2.1 collective-permute-start.9
  73.4 29.1 %banded_attention.5 = (f32[48,1024]{1,0:T(8,128)S(1)}, f32[32,1024]{1,0:T(8,128)S(1)}, f32[16,512]{1,0:T(8,128)S(1)}, f32[16,256]{1,0:T(8,128)S(1)}, f32[16,256]{1,0:T(8,128)S(1)}) custom-call(f32[1]{0:T(128)} %bitcast.bias_ref, f32[48,1024]{1,0:T(8,128)S(1)} %add.72.rank_ref, f32[32,1024]{1,0:T(8,128)S(1)} %copy-done.4, bf16[1024,2048]{1,0:T(8,128)(2,1)} %fq_ref.7, ...), custom_call_target="tpu_custom_call" | custom-call | flops 5368709120 | bytes 4194304 | tf_op jit(solution)/shard_map/banded_attention/pallas_call | solution.py:271
  102.5 29.0 %banded_attention.6 = (f32[48,1024]{1,0:T(8,128)S(1)}, f32[32,1024]{1,0:T(8,128)S(1)}, f32[16,512]{1,0:T(8,128)S(1)}, f32[16,256]{1,0:T(8,128)S(1)}, f32[16,256]{1,0:T(8,128)S(1)}) custom-call(f32[1]{0:T(128)} %bitcast.bias_ref, f32[48,1024]{1,0:T(8,128)S(1)} %add.72.rank_ref, f32[32,1024]{1,0:T(8,128)S(1)} %copy-done.4, bf16[1024,2048]{1,0:T(8,128)(2,1)} %fq_ref.7, ...), custom_call_target="tpu_custom_call" | custom-call | flops 5368709120 | bytes 4194304 | tf_op jit(solution)/shard_map/banded_attention/pallas_call | solution.py:271
  131.5 29.2 %banded_attention.7 = (f32[48,1024]{1,0:T(8,128)S(1)}, f32[32,1024]{1,0:T(8,128)S(1)}, f32[16,512]{1,0:T(8,128)S(1)}, f32[16,256]{1,0:T(8,128)S(1)}, f32[16,256]{1,0:T(8,128)S(1)}) custom-call(f32[1]{0:T(128)} %bitcast.bias_ref, f32[48,1024]{1,0:T(8,128)S(1)} %add.72.rank_ref, f32[32,1024]{1,0:T(8,128)S(1)} %copy-done.4, bf16[1024,2048]{1,0:T(8,128)(2,1)} %fq_ref.7, ...), custom_call_target="tpu_custom_call" | custom-call | flops 5368709120 | bytes 4194304 | tf_op jit(solution)/shard_map/banded_attention/pallas_call | solution.py:271
  162.1 3.0 %collective-permute-done.10 = f32[32,1024]{1,0:T(8,128)S(1)} collective-permute-done((f32[32,1024]{1,0:T(8,128)S(1)}, f32[32,1024]{1,0:T(8,128)S(1)}, u32[]{:S(2)}, u32[]{:S(2)}) %collective-permute-start.10) | collective-permute-done | bytes 131104 | tf_op jit(solution)/shard_map/ppermute | solution.py:293
  165.2 1.6 collective-permute-start.11
  166.7 4.2 %collective-permute-done.11 = f32[48,1024]{1,0:T(8,128)S(1)} collective-permute-done((f32[48,1024]{1,0:T(8,128)S(1)}, f32[48,1024]{1,0:T(8,128)S(1)}, u32[]{:S(2)}, u32[]{:S(2)}) %collective-permute-start.11) | collective-permute-done | bytes 196640 | tf_op jit(solution)/shard_map/ppermute | solution.py:303
  170.9 4.5 %fusion = f32[144,2688]{1,0:T(8,128)S(1)} fusion(bf16[2688,1024]{1,0:T(8,128)(2,1)} %param.11, bf16[48,1024]{1,0:T(8,128)(2,1)S(1)} %get-tuple-element.65, bf16[48,1024]{1,0:T(8,128)(2,1)S(1)} %get-tuple-element.64, bf16[48,1024]{1,0:T(8,128)(2,1)S(1)} %get-tuple-element.63), kind=kOutput, calls=%fused_computation.7 | convolution fusion | flops 793608192 | bytes 7348224 | tf_op jit(solution)/shard_map/dot_general | solution.py:391
  175.8 2.8 %collective-permute-start.12 = (f32[16,6144]{1,0:T(8,128)S(1)}, f32[16,6144]{1,0:T(8,128)S(1)}, u32[]{:S(2)}, u32[]{:S(2)}) collective-permute-start(f32[16,6144]{1,0:T(8,128)S(1)} %slice_select_fusion), channel_id=1, source_target_pairs={{0,2},{2,0},{4,6},{6,4},{8,10},{10,8},{12,14},{14,12},{16,18},{18,... | collective-permute-start | bytes 1179656 | tf_op jit(solution)/shard_map/ppermute | solution.py:321
  180.0 2.6 %collective-permute-start.13 = (f32[16,3072]{1,0:T(8,128)S(1)}, f32[16,3072]{1,0:T(8,128)S(1)}, u32[]{:S(2)}, u32[]{:S(2)}) collective-permute-start(f32[16,3072]{1,0:T(8,128)S(1)} %slice_select_fusion.1), channel_id=1, source_target_pairs={{0,4},{2,6},{4,0},{6,2},{8,12},{10,14},{12,8},{14,10},{16,20},{18,... | collective-permute-start | bytes 589832 | tf_op jit(solution)/shard_map/ppermute | solution.py:321
  182.6 5.4 %collective-permute-done.13 = f32[16,3072]{1,0:T(8,128)S(1)} collective-permute-done((f32[16,3072]{1,0:T(8,128)S(1)}, f32[16,3072]{1,0:T(8,128)S(1)}, u32[]{:S(2)}, u32[]{:S(2)}) %collective-permute-start.13) | collective-permute-done | bytes 196640 | tf_op jit(solution)/shard_map/ppermute | solution.py:321
  188.1 3.0 %collective-permute-start.14 = (f32[16,1536]{1,0:T(8,128)S(1)}, f32[16,1536]{1,0:T(8,128)S(1)}, u32[]{:S(2)}, u32[]{:S(2)}) collective-permute-start(f32[16,1536]{1,0:T(8,128)S(1)} %slice_select_fusion.2), channel_id=1, source_target_pairs={{0,8},{2,10},{4,12},{6,14},{8,0},{10,2},{12,4},{14,6},{16,24},{18,... | collective-permute-start | bytes 294920 | tf_op jit(solution)/shard_map/ppermute | solution.py:321
  191.1 2.6 %collective-permute-done.14 = f32[16,1536]{1,0:T(8,128)S(1)} collective-permute-done((f32[16,1536]{1,0:T(8,128)S(1)}, f32[16,1536]{1,0:T(8,128)S(1)}, u32[]{:S(2)}, u32[]{:S(2)}) %collective-permute-start.14) | collective-permute-done | bytes 98336 | tf_op jit(solution)/shard_map/ppermute | solution.py:321
  193.8 1.5 collective-permute-start.15
  195.2 3.6 %collective-permute-done.15 = f32[16,768]{1,0:T(8,128)S(1)} collective-permute-done((f32[16,768]{1,0:T(8,128)S(1)}, f32[16,768]{1,0:T(8,128)S(1)}, u32[]{:S(2)}, u32[]{:S(2)}) %collective-permute-start.15) | collective-permute-done | bytes 49184 | tf_op jit(solution)/shard_map/ppermute | solution.py:321
  200.3 3.7 %collective-permute-done.16 = f32[16,768]{1,0:T(8,128)S(1)} collective-permute-done((f32[16,768]{1,0:T(8,128)S(1)}, f32[16,768]{1,0:T(8,128)S(1)}, u32[]{:S(2)}, u32[]{:S(2)}) %collective-permute-start.16) | collective-permute-done | bytes 49184 | tf_op jit(solution)/shard_map/ppermute | solution.py:327
  204.0 2.1 collective-permute-start.17
  206.1 2.6 %collective-permute-done.17 = f32[16,1536]{1,0:T(8,128)S(1)} collective-permute-done((f32[16,1536]{1,0:T(8,128)S(1)}, f32[16,1536]{1,0:T(8,128)S(1)}, u32[]{:S(2)}, u32[]{:S(2)}) %collective-permute-start.17) | collective-permute-done | bytes 98336 | tf_op jit(solution)/shard_map/ppermute | solution.py:327
  209.7 4.8 %collective-permute-done.18 = f32[16,3072]{1,0:T(8,128)S(1)} collective-permute-done((f32[16,3072]{1,0:T(8,128)S(1)}, f32[16,3072]{1,0:T(8,128)S(1)}, u32[]{:S(2)}, u32[]{:S(2)}) %collective-permute-start.18) | collective-permute-done | bytes 196640 | tf_op jit(solution)/shard_map/ppermute | solution.py:327
  214.6 1.7 collective-permute-done.19
  (89 shorter events, 15.6 us)
Async XLA Ops:
  0.6 5.7 %copy-start.1 = (bf16[1024,1024]{1,0:T(8,128)(2,1)S(1)}, bf16[1024,1024]{1,0:T(8,128)(2,1)}, u32[]{:S(2)}) copy-start(bf16[1024,1024]{1,0:T(8,128)(2,1)} %fv_ref.7) | copy-start | bytes 6291460
  0.6 11.7 %copy-start.10 = (bf16[2688,1024]{1,0:T(8,128)(2,1)S(1)}, bf16[2688,1024]{1,0:T(8,128)(2,1)}, u32[]{:S(2)}) copy-start(bf16[2688,1024]{1,0:T(8,128)(2,1)} %param.11) | copy-start | bytes 16515076
  0.7 11.7 %copy-start.14 = (bf16[2688,16]{0,1:T(8,128)(2,1)S(1)}, bf16[2688,16]{0,1:T(8,128)(2,1)}, u32[]{:S(2)}) copy-start(bf16[2688,16]{0,1:T(8,128)(2,1)} %param.16) | copy-start | bytes 258052
  0.7 11.7 %copy-start.13 = (bf16[2688,16]{0,1:T(8,128)(2,1)S(1)}, bf16[2688,16]{0,1:T(8,128)(2,1)}, u32[]{:S(2)}) copy-start(bf16[2688,16]{0,1:T(8,128)(2,1)} %param.18) | copy-start | bytes 258052
  0.7 11.7 %copy-start.12 = (bf16[2688,16]{0,1:T(8,128)(2,1)S(1)}, bf16[2688,16]{0,1:T(8,128)(2,1)}, u32[]{:S(2)}) copy-start(bf16[2688,16]{0,1:T(8,128)(2,1)} %param.20) | copy-start | bytes 258052
  3.7 28.9 %collective-permute-start.2 = (bf16[1024,256]{1,0:T(8,128)(2,1)}, bf16[1024,256]{1,0:T(8,128)(2,1)S(1)}, u32[]{:S(2)}, u32[]{:S(2)}) collective-permute-start(bf16[1024,256]{1,0:T(8,128)(2,1)} %get-tuple-element.52), channel_id=1, source_target_pairs={{0,2},{2,4},{4,6},{6,8},{8,10},{10,12},{12,14},{14,16},{16,18},{18... | collective-permute-start | bytes 1572872 | tf_op jit(solution)/shard_map/ppermute | solution.py:293
  7.7 30.4 %copy-start = (bf16[1024,1024]{1,0:T(8,128)(2,1)S(1)}, bf16[1024,1024]{1,0:T(8,128)(2,1)}, u32[]{:S(2)}) copy-start(bf16[1024,1024]{1,0:T(8,128)(2,1)} %fk_ref.7) | copy-start | bytes 6291460
  7.7 30.5 %copy-start.7 = (bf16[16,1024]{1,0:T(8,128)(2,1)S(1)}, bf16[16,1024]{1,0:T(8,128)(2,1)}, u32[]{:S(2)}) copy-start(bf16[16,1024]{1,0:T(8,128)(2,1)} %uk_ref.7) | copy-start | bytes 98308
  7.7 26.9 %collective-permute-start.3 = (bf16[1024,256]{1,0:T(8,128)(2,1)}, bf16[1024,256]{1,0:T(8,128)(2,1)S(1)}, u32[]{:S(2)}, u32[]{:S(2)}) collective-permute-start(bf16[1024,256]{1,0:T(8,128)(2,1)} %get-tuple-element.48), channel_id=1, source_target_pairs={{0,2},{2,4},{4,6},{6,8},{8,10},{10,12},{12,14},{14,16},{16,18},{18... | collective-permute-start | bytes 1572872 | tf_op jit(solution)/shard_map/ppermute | solution.py:293
  13.5 6.9 %collective-permute-start = (f32[48,1024]{1,0:T(8,128)S(1)}, f32[48,1024]{1,0:T(8,128)S(1)}, u32[]{:S(2)}, u32[]{:S(2)}) collective-permute-start(f32[48,1024]{1,0:T(8,128)S(1)} %fusion.6), channel_id=1, source_target_pairs={{0,1},{1,0},{2,3},{3,2},{4,5},{5,4},{6,7},{7,6},{8,9},{9,8},{10,11... | collective-permute-start | bytes 589832 | tf_op jit(solution)/shard_map/ppermute | solution.py:303
  21.0 8.4 %collective-permute-start.1 = (f32[32,1024]{1,0:T(8,128)}, f32[32,1024]{1,0:T(8,128)S(1)}, u32[]{:S(2)}, u32[]{:S(2)}) collective-permute-start(f32[32,1024]{1,0:T(8,128)} %slice.125), channel_id=1, source_target_pairs={{0,2},{2,4},{4,6},{6,8},{8,10},{10,12},{12,14},{14,16},{16,18},{18... | collective-permute-start | bytes 393224 | tf_op jit(solution)/shard_map/ppermute | solution.py:293
  22.3 48.9 %collective-permute-start.4 = (bf16[1024,256]{1,0:T(8,128)(2,1)}, bf16[1024,256]{1,0:T(8,128)(2,1)}, u32[]{:S(2)}, u32[]{:S(2)}) collective-permute-start(bf16[1024,256]{1,0:T(8,128)(2,1)} %get-tuple-element.50), channel_id=1, source_target_pairs={{0,2},{2,4},{4,6},{6,8},{8,10},{10,12},{12,14},{14,16},{16,18},{18... | collective-permute-start | bytes 1572872 | tf_op jit(solution)/shard_map/ppermute | solution.py:293
  27.3 46.1 %collective-permute-start.5 = (bf16[1024,256]{1,0:T(8,128)(2,1)}, bf16[1024,256]{1,0:T(8,128)(2,1)}, u32[]{:S(2)}, u32[]{:S(2)}) collective-permute-start(bf16[1024,256]{1,0:T(8,128)(2,1)} %get-tuple-element.46), channel_id=1, source_target_pairs={{0,2},{2,4},{4,6},{6,8},{8,10},{10,12},{12,14},{14,16},{16,18},{18... | collective-permute-start | bytes 1572872 | tf_op jit(solution)/shard_map/ppermute | solution.py:293
  30.1 72.5 %collective-permute-start.6 = (bf16[1024,256]{1,0:T(8,128)(2,1)}, bf16[1024,256]{1,0:T(8,128)(2,1)S(1)}, u32[]{:S(2)}, u32[]{:S(2)}) collective-permute-start(bf16[1024,256]{1,0:T(8,128)(2,1)} %get-tuple-element.51), channel_id=1, source_target_pairs={{0,2},{2,4},{4,6},{6,8},{8,10},{10,12},{12,14},{14,16},{16,18},{18... | collective-permute-start | bytes 1572872 | tf_op jit(solution)/shard_map/ppermute | solution.py:293
  32.6 69.9 %collective-permute-start.7 = (bf16[1024,256]{1,0:T(8,128)(2,1)}, bf16[1024,256]{1,0:T(8,128)(2,1)S(1)}, u32[]{:S(2)}, u32[]{:S(2)}) collective-permute-start(bf16[1024,256]{1,0:T(8,128)(2,1)} %get-tuple-element.47), channel_id=1, source_target_pairs={{0,2},{2,4},{4,6},{6,8},{8,10},{10,12},{12,14},{14,16},{16,18},{18... | collective-permute-start | bytes 1572872 | tf_op jit(solution)/shard_map/ppermute | solution.py:293
  34.6 96.9 %collective-permute-start.8 = (bf16[1024,256]{1,0:T(8,128)(2,1)}, bf16[1024,256]{1,0:T(8,128)(2,1)S(1)}, u32[]{:S(2)}, u32[]{:S(2)}) collective-permute-start(bf16[1024,256]{1,0:T(8,128)(2,1)} %get-tuple-element.53), channel_id=1, source_target_pairs={{0,2},{2,4},{4,6},{6,8},{8,10},{10,12},{12,14},{14,16},{16,18},{18... | collective-permute-start | bytes 1572872 | tf_op jit(solution)/shard_map/ppermute | solution.py:293
  38.1 1.6 copy-start.2
  39.7 0.9 copy-start.4
  42.2 29.0 %copy-start.11 = (bf16[1024,256]{1,0:T(8,128)(2,1)S(1)}, bf16[1024,256]{1,0:T(8,128)(2,1)}, u32[]{:S(2)}) copy-start(bf16[1024,256]{1,0:T(8,128)(2,1)} %get-tuple-element.49) | copy-start | bytes 1572868
  42.2 31.1 %copy-start.6 = (bf16[16,2048]{1,0:T(8,128)(2,1)S(1)}, bf16[16,2048]{1,0:T(8,128)(2,1)}, u32[]{:S(2)}) copy-start(bf16[16,2048]{1,0:T(8,128)(2,1)} %uq_ref.7) | copy-start | bytes 196612
  71.3 60.3 %collective-permute-start.9 = (bf16[1024,256]{1,0:T(8,128)(2,1)S(1)}, bf16[1024,256]{1,0:T(8,128)(2,1)S(1)}, u32[]{:S(2)}, u32[]{:S(2)}) collective-permute-start(bf16[1024,256]{1,0:T(8,128)(2,1)S(1)} %copy-done.11), channel_id=1, source_target_pairs={{0,2},{2,4},{4,6},{6,8},{8,10},{10,12},{12,14},{14,16},{16,18},{18... | collective-permute-start | bytes 1572872 | tf_op jit(solution)/shard_map/ppermute | solution.py:293
  102.5 29.0 %copy-start.9 = (bf16[16,1024]{1,0:T(8,128)(2,1)S(1)}, bf16[16,1024]{1,0:T(8,128)(2,1)}, u32[]{:S(2)}) copy-start(bf16[16,1024]{1,0:T(8,128)(2,1)} %uv_ref.7) | copy-start | bytes 98308
  160.8 4.3 %collective-permute-start.10 = (f32[32,1024]{1,0:T(8,128)S(1)}, f32[32,1024]{1,0:T(8,128)S(1)}, u32[]{:S(2)}, u32[]{:S(2)}) collective-permute-start(f32[32,1024]{1,0:T(8,128)S(1)} %add_add_fusion.1), channel_id=1, source_target_pairs={{2,0},{4,2},{6,4},{8,6},{10,8},{12,10},{14,12},{16,14},{18,16},{20... | collective-permute-start | bytes 393224 | tf_op jit(solution)/shard_map/ppermute | solution.py:293
  165.2 5.7 %collective-permute-start.11 = (f32[48,1024]{1,0:T(8,128)S(1)}, f32[48,1024]{1,0:T(8,128)S(1)}, u32[]{:S(2)}, u32[]{:S(2)}) collective-permute-start(f32[48,1024]{1,0:T(8,128)S(1)} %pad_maximum_fusion.1), channel_id=1, source_target_pairs={{0,1},{1,0},{2,3},{3,2},{4,5},{5,4},{6,7},{7,6},{8,9},{9,8},{10,11... | collective-permute-start | bytes 589832 | tf_op jit(solution)/shard_map/ppermute | solution.py:303
  175.8 4.1 %collective-permute-start.12 = (f32[16,6144]{1,0:T(8,128)S(1)}, f32[16,6144]{1,0:T(8,128)S(1)}, u32[]{:S(2)}, u32[]{:S(2)}) collective-permute-start(f32[16,6144]{1,0:T(8,128)S(1)} %slice_select_fusion), channel_id=1, source_target_pairs={{0,2},{2,0},{4,6},{6,4},{8,10},{10,8},{12,14},{14,12},{16,18},{18,... | collective-permute-start | bytes 1179656 | tf_op jit(solution)/shard_map/ppermute | solution.py:321
  180.0 8.0 %collective-permute-start.13 = (f32[16,3072]{1,0:T(8,128)S(1)}, f32[16,3072]{1,0:T(8,128)S(1)}, u32[]{:S(2)}, u32[]{:S(2)}) collective-permute-start(f32[16,3072]{1,0:T(8,128)S(1)} %slice_select_fusion.1), channel_id=1, source_target_pairs={{0,4},{2,6},{4,0},{6,2},{8,12},{10,14},{12,8},{14,10},{16,20},{18,... | collective-permute-start | bytes 589832 | tf_op jit(solution)/shard_map/ppermute | solution.py:321
  188.1 5.6 %collective-permute-start.14 = (f32[16,1536]{1,0:T(8,128)S(1)}, f32[16,1536]{1,0:T(8,128)S(1)}, u32[]{:S(2)}, u32[]{:S(2)}) collective-permute-start(f32[16,1536]{1,0:T(8,128)S(1)} %slice_select_fusion.2), channel_id=1, source_target_pairs={{0,8},{2,10},{4,12},{6,14},{8,0},{10,2},{12,4},{14,6},{16,24},{18,... | collective-permute-start | bytes 294920 | tf_op jit(solution)/shard_map/ppermute | solution.py:321
  193.8 5.1 %collective-permute-start.15 = (f32[16,768]{1,0:T(8,128)S(1)}, f32[16,768]{1,0:T(8,128)S(1)}, u32[]{:S(2)}, u32[]{:S(2)}) collective-permute-start(f32[16,768]{1,0:T(8,128)S(1)} %slice_select_fusion.3), channel_id=1, source_target_pairs={{0,16},{2,18},{4,20},{6,22},{8,24},{10,26},{12,28},{14,30},{16,0},... | collective-permute-start | bytes 147464 | tf_op jit(solution)/shard_map/ppermute | solution.py:321
  198.8 5.2 %collective-permute-start.16 = (f32[16,768]{1,0:T(8,128)S(1)}, f32[16,768]{1,0:T(8,128)S(1)}, u32[]{:S(2)}, u32[]{:S(2)}) collective-permute-start(f32[16,768]{1,0:T(8,128)S(1)} %select_add_fusion.3), channel_id=1, source_target_pairs={{0,16},{2,18},{4,20},{6,22},{8,24},{10,26},{12,28},{14,30},{16,0},... | collective-permute-start | bytes 147464 | tf_op jit(solution)/shard_map/ppermute | solution.py:327
  204.0 4.7 %collective-permute-start.17 = (f32[16,1536]{1,0:T(8,128)S(1)}, f32[16,1536]{1,0:T(8,128)S(1)}, u32[]{:S(2)}, u32[]{:S(2)}) collective-permute-start(f32[16,1536]{1,0:T(8,128)S(1)} %pad_maximum_fusion.4), channel_id=1, source_target_pairs={{0,8},{2,10},{4,12},{6,14},{8,0},{10,2},{12,4},{14,6},{16,24},{18,... | collective-permute-start | bytes 294920 | tf_op jit(solution)/shard_map/ppermute | solution.py:327
  208.7 5.7 %collective-permute-start.18 = (f32[16,3072]{1,0:T(8,128)S(1)}, f32[16,3072]{1,0:T(8,128)S(1)}, u32[]{:S(2)}, u32[]{:S(2)}) collective-permute-start(f32[16,3072]{1,0:T(8,128)S(1)} %pad_maximum_fusion.2), channel_id=1, source_target_pairs={{0,4},{2,6},{4,0},{6,2},{8,12},{10,14},{12,8},{14,10},{16,20},{18,... | collective-permute-start | bytes 589832 | tf_op jit(solution)/shard_map/ppermute | solution.py:327
  214.5 1.8 collective-permute-start.19
  (3 other events, 2.3 us)
